TPU v7x, 32 devices: a whole 2x2x4 slice. The times are simulated.
32 devices in a mesh: grp: 2 (over x), ha: 8 (over z, y), col: 2 (over core).
Axes of the slice: x: 2, y: 2, z: 4, core: 2. Of those that a mesh axis runs over, the one named last changes fastest.
Arguments:
- latent: bfloat16 [2, 64, 128, 384], P('grp', 'ha', None, 'col'), parts along dimension 0, may hold values from -6 to 6
- up_weight: bfloat16 [4, 4, 384, 192], replicated, may hold values from -0.15625 to 0.15625
- conv_one: bfloat16 [3, 3, 192, 192], replicated, may hold values from -0.15625 to 0.15625
- gain_one: float32 [192], replicated, may hold values from 0.1 to 1.9
- conv_two: bfloat16 [3, 3, 192, 192], replicated, may hold values from -0.15625 to 0.15625
- gain_two: float32 [192], replicated, may hold values from 0.1 to 1.9
Outputs:
- decoded: bfloat16 [2, 128, 256, 192], P('grp', 'ha', 'col'), parts along dimension 0
There are 2 independent parts, one for each index of `grp`. A program takes and returns all parts, laid end to end along the dimension named above; an argument that names none is the same for every part. Nothing has to cross between parts.
All inputs are finite; a program needn't handle non-finite values.
Results may differ from a plain program's by a relative error of at most 0.008.
Values may be sent and summed in bfloat16 or wider, within the bound.
A program may use at most 64 MiB of HBM per device.

v0:
```python
import functools

import jax
import jax.numpy as jnp
from jax import lax
from jax.experimental import pallas as pl
from jax.experimental.pallas import tpu as pltpu
from jax.sharding import PartitionSpec as P

f32 = jnp.float32
bf16 = jnp.bfloat16
MESH = pl.DeviceIdType.MESH
SLOT = 8
SLOT_AT = 3
phase_taps = (((0, 1), (-1, 3)), ((0, 2), (1, 0)))


def activate(wide, half_gain):
    stats = jnp.sum(wide * wide, axis=0, keepdims=True) * (1.0 / wide.shape[0])
    half = wide * lax.rsqrt(stats + 1e-06) * half_gain
    return half * jnp.tanh(half) + half


def block_kernel(
    ha_count, lat, gain_one, gain_two, up_hbm, one_hbm, two_hbm, out, two_w, ups, second,
    up_w, raw, one_w, field, pairs, first, gains, perm,
    slim, sem, send, recv
):
    ha = lax.axis_index("ha")
    col = lax.axis_index("col")
    rows, share, width = lat.shape[1], lat.shape[2], lat.shape[3]
    chans = out.shape[2]
    half = width // 2
    depth = 2 * share
    mine = pl.ds(pl.multiple_of(col * share, share), share)
    other = {"col": 1 - col}
    has_above, has_below = ha > 0, ha < ha_count - 1

    barrier = pltpu.get_barrier_semaphore()
    pl.semaphore_signal(barrier, 1, device_id=other, device_id_type=MESH)

    @pl.when(has_above)
    def _():
        pl.semaphore_signal(barrier, 1, device_id={"ha": ha - 1}, device_id_type=MESH)

    @pl.when(has_below)
    def _():
        pl.semaphore_signal(barrier, 1, device_id={"ha": ha + 1}, device_id_type=MESH)

    own = pltpu.make_async_copy(lat.at[0], field.at[pl.ds(2, rows), mine], sem.at[0])
    own.start()
    raw_copies = [
        pltpu.make_async_copy(src, raw.at[n], sem.at[1 + n])
        for n, src in enumerate((one_hbm, two_hbm))
    ]
    for item in raw_copies:
        item.start()
    up_copies = []
    for rp in range(2):
        for cp in range(2):
            tap = 0
            for _, ra in phase_taps[rp]:
                for _, cb in phase_taps[cp]:
                    up_copies.append(pltpu.make_async_copy(
                        up_hbm.at[ra, cb],
                        up_w.at[rp, cp, :, pl.ds(tap * depth, depth)],
                        sem.at[3],
                    ))
                    tap += 1
    for item in up_copies:
        item.start()

    peers = 1 + jnp.minimum(ha, 1) + jnp.minimum(ha_count - 1 - ha, 1)
    pl.semaphore_wait(barrier, peers)

    def remote(src, dst, target, n):
        return pltpu.make_async_remote_copy(
            src_ref=src, dst_ref=dst, send_sem=send.at[n], recv_sem=recv.at[n],
            device_id=target, device_id_type=MESH,
        )

    side = remote(lat.at[0], field.at[pl.ds(2, rows), mine], other, 0)
    downs, ups_sent, pass_tops, pass_bottoms = [], [], [], []
    for n in range(2):
        top, bottom = field.at[1 - n, mine], field.at[rows + 2 + n, mine]
        downs.append(remote(lat.at[0, rows - 1 - n], top, {"ha": ha + 1}, 1 + n))
        ups_sent.append(remote(lat.at[0, n], bottom, {"ha": ha - 1}, 3 + n))
        pass_tops.append(remote(top, top, other, 5 + n))
        pass_bottoms.append(remote(bottom, bottom, other, 7 + n))

    for n in range(2):
        @pl.when(has_below)
        def _():
            downs[n].start()

        @pl.when(has_above)
        def _():
            ups_sent[n].start()

    side.start()

    @pl.when(ha == 0)
    def _():
        field[pl.ds(0, 2)] = jnp.zeros((2, depth, width), bf16)

    @pl.when(ha == ha_count - 1)
    def _():
        field[pl.ds(rows + 2, 2)] = jnp.zeros((2, depth, width), bf16)

    for n, gain in enumerate((gain_one, gain_two)):
        gains[n] = jnp.broadcast_to(gain[...] * 0.5, (width, chans)).T
    at = lax.broadcasted_iota(jnp.int32, (2 * width, 2 * width), 0)
    to = lax.broadcasted_iota(jnp.int32, (2 * width, 2 * width), 1)
    source = (to % 2) * width + (to // width) * half + (to % width) // 2
    perm[...] = (source == at).astype(f32).astype(bf16)

    def turn(n, turned):
        at = lax.broadcasted_iota(jnp.int32, (chans, chans), 0)
        to = lax.broadcasted_iota(jnp.int32, (chans, chans), 1)
        eye = (at == to).astype(f32).astype(bf16)
        taps = [raw[n, a, b] for a in range(3) for b in (2 - 2 * col, 1, 2 * col)]
        turned[...] = lax.dot_general(
            eye, jnp.concatenate(taps, axis=0), (((1,), (1,)), ((), ())),
            preferred_element_type=f32,
        ).astype(bf16)

    lane = lax.broadcasted_iota(jnp.int32, (share, width), 1)
    keep_near = (lane < half) == (col == 0)
    low = lane % half == 0
    high = lane % half == half - 1
    low_col = low & (col == 0)
    high_col = high & (col > 0)
    zero = jnp.zeros((share, width), bf16)

    def store_planes(n, here, there, part):
        pairs[n, 1, part] = here
        pairs[n, 0, part] = pltpu.roll(
            jnp.where(high_col, there, jnp.where(high, zero, here)), 1, 1
        )
        pairs[n, 2, part] = pltpu.roll(
            jnp.where(low_col, there, jnp.where(low, zero, here)), width - 1, 1
        )

    def halves(f, apart, part):
        near = field[f + apart * col, part]
        far = pltpu.roll(field[f + apart * (1 - col), part], half, 1)
        return jnp.where(keep_near, near, far), jnp.where(keep_near, far, near)

    def make_pair(n, f, apart, part):
        here, there = halves(f, apart, part)
        store_planes(n, here, there, part)

    def halo_slots(listed, part):
        total = zero
        for s, f in enumerate(listed):
            moved = pltpu.roll(field[f, part], SLOT * s + SLOT_AT + col, 1)
            total = jnp.where(lane // SLOT == half // SLOT + s, moved, total)
        return total

    cell = lax.broadcasted_iota(jnp.int32, (chans, width), 1)
    blank = jnp.zeros((chans, width), bf16)
    inward = 1 + (1 - col) * (width - 2)
    outward = 1 + col * (width - 2)
    joint_cell = cell == (1 - col) * (width - 1)
    rim_cell = cell == col * (width - 1)

    def place(field3, r, value, moved):
        turned_in = pltpu.roll(value, inward, 1)
        if moved is not None:
            turned_in = jnp.where(joint_cell, moved, turned_in)
        field3[r, pl.ds(chans, chans)] = value
        field3[r, pl.ds(0, chans)] = turned_in
        field3[r, pl.ds(2 * chans, chans)] = jnp.where(
            rim_cell, blank, pltpu.roll(value, outward, 1)
        )

    def framed(r, value):
        if r < 2:
            return jnp.where(has_above, value, jnp.zeros_like(value))
        if r >= 2 * rows + 2:
            return jnp.where(has_below, value, jnp.zeros_like(value))
        return value

    def upsample(plane, count, plan, apart):
        extras = []
        parts = {}

        def phase(rp, cp):
            pieces = [
                jnp.concatenate([plane(rp, k, dr + 1 - rp, dc) for k in range(count)], axis=1)
                for dr, _ in phase_taps[rp] for dc, _ in phase_taps[cp]
            ]
            parts[rp, cp] = jnp.dot(
                up_w[rp, cp], jnp.concatenate(pieces, axis=0), preferred_element_type=f32
            ).astype(bf16)

        if apart:
            for cp in range(2):
                for rp in range(2):
                    phase(rp, cp)
        for rp in range(2):
            if not apart:
                phase(rp, 0)
                phase(rp, 1)
            extra = None
            for k in (count - 1, *range(count - 1)):
                cut = slice(k * width, (k + 1) * width)
                both = jnp.concatenate([parts[rp, 0][:, cut], parts[rp, 1][:, cut]], axis=1)
                mixed = jnp.dot(both, perm[...], preferred_element_type=f32)
                todo = plan(rp, k)
                for side_half in sorted(range(2), key=lambda x: todo[x] != "halo"):
                    value = mixed[:, side_half * width:(side_half + 1) * width]
                    act = activate(value, gains[0]).astype(bf16)
                    if todo[side_half] == "halo":
                        extra = act
                        continue
                    r, slot = todo[side_half]
                    if 2 <= r < 2 * rows + 2:
                        ups[r - 2] = value.astype(bf16)
                    moved = pltpu.roll(extra, width - 1 - 2 * SLOT_AT - 2 * SLOT * slot, 1)
                    place(first, r, framed(r, act), framed(r, moved))
            extras.append(extra)
        return extras

    def windows(field3, span):
        return jnp.concatenate(
            [field3[pl.ds(r, 3)].reshape(9 * chans, width) for r in span], axis=1
        )

    def slim_near_far(first_half, second_half, apart):
        return [
            jnp.where(
                cell % (2 * SLOT) == SLOT - 1,
                pltpu.roll(first_half, shift, 1),
                pltpu.roll(second_half, apart + shift, 1),
            )
            for shift in (col, 1 - col)
        ]

    def slim_edges(listed):
        total = blank
        for r, s in listed:
            moved = pltpu.roll(first[r, pl.ds(chans, chans)], SLOT * s + SLOT - col, 1)
            total = jnp.where(cell // SLOT == s, moved, total)
        return total

    def slim_windows(slims):
        return jnp.concatenate(
            [pltpu.roll(x, (SLOT * (1 - d)) % width, 1) if d != 1 else x
             for d in range(3) for x in slims], axis=0
        )

    def normed(total):
        return activate(total.astype(bf16).astype(f32), gains[1])

    def conv_one(span, slims, slot_of):
        totals = {}
        for group in span:
            rhs = jnp.concatenate([
                slim_windows(slims) if r is None else
                first[pl.ds(r, 3)].reshape(9 * chans, width) for r in group
            ], axis=1)
            total = jnp.dot(one_w[...], rhs, preferred_element_type=f32)
            for k, r in enumerate(group):
                totals[r] = total[:, k * width:(k + 1) * width]
        joint = normed(totals[None]).astype(bf16)
        for group in span:
            for r in group:
                if r is None:
                    continue
                act = normed(totals[r]).astype(bf16)
                moved = pltpu.roll(joint, width - SLOT * (slot_of(r) + 1) + col, 1)
                if r == 0 or r == 2 * rows + 1:
                    inside = has_above if r == 0 else has_below
                    act = jnp.where(inside, act, blank)
                    moved = jnp.where(inside, moved, blank)
                place(second, r, act, moved)

    def conv_two(span):
        total = jnp.dot(two_w[...], windows(second, span), preferred_element_type=f32)
        for k, r in enumerate(span):
            value = total[:, k * width:(k + 1) * width] + ups[r].astype(f32)
            out[0, r] = value.astype(bf16)

    def forward(n):
        @pl.when(has_above)
        def _():
            downs[n].wait_recv()
            pass_tops[n].start()

        @pl.when(has_below)
        def _():
            ups_sent[n].wait_recv()
            pass_bottoms[n].start()

    def arrived(n):
        @pl.when(has_above)
        def _():
            ups_sent[n].wait_send()
            pass_tops[n].wait()

        @pl.when(has_below)
        def _():
            downs[n].wait_send()
            pass_bottoms[n].wait()

    h = rows // 2
    theirs = pl.ds(pl.multiple_of((1 - col) * share, share), share)
    base = h + 2

    def inner_pairs(part):
        for k in range(h):
            make_pair(k, 2 + k, h, part)
        slots = halo_slots(range(2, rows + 2), part)
        for k in range(2):
            here, there = halves(1 + h + k, 0, part)
            here = jnp.where(lane < half, here, slots)
            store_planes(h + k, here, there, part)
            slots = pltpu.roll(slots, width - SLOT, 1)

    def inner_plane(rp, k, step, dc):
        return pairs[k + step if k < h - 1 else h + step, 1 + dc]

    def inner_plan(rp, k):
        r = 4 - rp + 2 * k
        if k == h - 1:
            return (r, k), "halo"
        return (r, k), (r + 2 * h, k + h)

    def outer_pairs(part):
        for k in range(3):
            make_pair(base + k, k, rows + 1, part)
        slots = halo_slots((0, 1, 2, 2, rows + 1, rows + 2, rows + 3), part)
        slots = jnp.where(lane < half, pltpu.roll(slots, half, 1), slots)
        for k in range(2):
            store_planes(base + 3 + k, slots, slots, part)
            slots = pltpu.roll(slots, width - SLOT, 1)

    full_lane = lax.broadcasted_iota(jnp.int32, (depth, width), 1) < half

    def outer_plane(rp, k, step, dc):
        if k == 0:
            return pairs[base + rp + step, 1 + dc]
        slots = pairs[base + 3 + step, 1 + dc]
        if rp == 0:
            return jnp.where(full_lane, pairs[base + 1 + step, 1 + dc], slots)
        return jnp.where(full_lane, slots, pairs[base + step, 1 + dc])

    def outer_plan(rp, k):
        if k == 0:
            return (rp, rp), (2 * rows + 2 + rp, 4 + rp)
        return ((2, 1), "halo") if rp == 0 else ("halo", (2 * rows + 1, 4))

    own.wait()
    inner_pairs(mine)
    raw_copies[0].wait()
    turn(0, one_w)
    raw_copies[1].wait()
    side.wait()
    inner_pairs(theirs)
    for item in up_copies:
        item.wait()

    extras = upsample(inner_plane, h, inner_plan, False)
    slims = slim_near_far(extras[1], extras[0], SLOT)
    slims.append(slim_edges([(r, r - 3) for r in range(3, 2 * rows + 1)]))
    for n in range(3):
        slim[n] = slims[n]
    turn(1, two_w)
    conv_one(
        (range(3, 7), (None, 7, 8, 9), range(10, 2 * rows - 1)), slims, lambda r: r - 2
    )
    forward(0)
    forward(1)
    outer_pairs(mine)
    conv_two(range(3, 7))
    conv_two(range(7, 11))
    conv_two(range(11, 2 * rows - 3))
    arrived(0)
    arrived(1)
    outer_pairs(theirs)
    extras = upsample(outer_plane, 2, outer_plan, True)
    slims = slim_near_far(extras[0], extras[1], width - SLOT)
    slims.append(slim_edges([
        *((r, r) for r in range(5)), *((2 * rows - 1 + r, 5 + r) for r in range(5))
    ]))
    spot = cell // SLOT
    gone = ((spot < 2) & (ha == 0)) | ((spot >= 8) & (ha == ha_count - 1))
    for n in range(2):
        value = jnp.where(gone, blank, slims[n])
        value = jnp.where(spot == 3, pltpu.roll(slim[n], 3 * SLOT, 1), value)
        value = jnp.where(spot == 4, pltpu.roll(slim[n], 3 * SLOT, 1), value)
        old = pltpu.roll(slim[n], width - (2 * rows - 9) * SLOT, 1)
        slims[n] = jnp.where((spot == 5) | (spot == 6), old, value)
    conv_one(
        ((0, 1, 2, 2 * rows - 1), (None, 2 * rows, 2 * rows + 1)), slims,
        lambda r: r + 1 if r < 3 else r - (2 * rows - 7)
    )


def finish_kernel(ready, weight, skip, field3, dst, tail, sem):
    count, chans, width = skip.shape
    inner = pl.ds(3, count - 6)
    items = [pltpu.make_async_copy(ready.at[0, inner], dst.at[0, inner], sem.at[0])]
    items[0].start()
    spans = ((0, 1, 2), (count - 3, count - 2, count - 1))
    for n, span in enumerate(spans):
        spot = pl.ds(span[0], 3)
        items.append(pltpu.make_async_copy(tail.at[n], dst.at[0, spot], sem.at[1 + n]))
    begun = 0
    for group in ((0, 1, 2, count - 3), (count - 2, count - 1)):
        rhs = jnp.concatenate(
            [field3[pl.ds(r, 3)].reshape(9 * chans, width) for r in group], axis=1
        )
        total = jnp.dot(weight[...], rhs, preferred_element_type=f32)
        for k, r in enumerate(group):
            value = total[:, k * width:(k + 1) * width] + skip[r].astype(f32)
            n = 0 if r < 3 else 1
            tail[n, r - spans[n][0]] = value.astype(bf16)
        begun += 1
        items[begun].start()
    for item in items:
        item.wait()


def local(ha_count, latent, up_weight, conv_one, gain_one, conv_two, gain_two):
    _, rows, width, share = latent.shape
    chans = conv_one.shape[3]
    latent = jnp.transpose(latent, (0, 1, 3, 2))
    up_weight = jnp.transpose(up_weight, (0, 1, 3, 2))
    anywhere = pl.BlockSpec(memory_space=pl.ANY)
    vmem = pl.BlockSpec(memory_space=pltpu.VMEM)
    depth = 2 * share
    result = pl.pallas_call(
        functools.partial(block_kernel, ha_count),
        out_shape=[
            pltpu.VMEM((1, 2 * rows, chans, width), bf16),
            pltpu.VMEM((chans, 9 * chans), bf16),
            pltpu.VMEM((2 * rows, chans, width), bf16),
            pltpu.VMEM((2 * rows + 2, 3 * chans, width), bf16),
        ],
        in_specs=[anywhere] + [vmem] * 2 + [anywhere] * 3,
        out_specs=[vmem] * 4,
        scratch_shapes=[
            pltpu.VMEM((2, 2, chans, 4 * depth), bf16),
            pltpu.VMEM((2, 3, 3, chans, chans), bf16),
            pltpu.VMEM((chans, 9 * chans), bf16),
            pltpu.VMEM((rows + 4, depth, width), bf16),
            pltpu.VMEM((rows // 2 + 7, 3, depth, width), bf16),
            pltpu.VMEM((2 * rows + 4, 3 * chans, width), bf16),
            pltpu.VMEM((2, chans, width), f32),
            pltpu.VMEM((2 * width, 2 * width), bf16),
            pltpu.VMEM((3, chans, width), bf16),
            pltpu.SemaphoreType.DMA((4,)),
            pltpu.SemaphoreType.DMA((9,)),
            pltpu.SemaphoreType.DMA((9,)),
        ],
        compiler_params=pltpu.CompilerParams(
            vmem_limit_bytes=56000000, collective_id=0, has_side_effects=True
        ),
    )(latent, gain_one.reshape(1, chans), gain_two.reshape(1, chans),
      up_weight, conv_one, conv_two)
    result = pl.pallas_call(
        finish_kernel,
        out_shape=jax.ShapeDtypeStruct(result[0].shape, bf16),
        in_specs=[vmem] * 4,
        out_specs=pl.BlockSpec(memory_space=pltpu.HBM),
        scratch_shapes=[
            pltpu.VMEM((2, 3, chans, width), bf16),
            pltpu.SemaphoreType.DMA((3,)),
        ],
        compiler_params=pltpu.CompilerParams(vmem_limit_bytes=8 * 1024 * 1024),
    )(*result)
    return jnp.transpose(result, (0, 1, 3, 2))


def solution(mesh):
    return jax.shard_map(
        functools.partial(local, mesh.shape["ha"]),
        mesh=mesh,
        in_specs=(P("grp", "ha", None, "col"), P(), P(), P(), P(), P()),
        out_specs=P("grp", "ha", "col", None),
        check_vma=False,
    )
```

profile of v0, /device:TPU:0, one launch (start us, length us, event | category | flops | bytes accessed | tf_op | source)
XLA Modules:
  0.0 15.5 jit_solution(5189455306844426452)
XLA Ops:
  0.0 14.1 %shard_map.64 = (bf16[1,16,192,128]{3,2,1,0:T(8,128)(2,1)S(1)}, bf16[192,1728]{1,0:T(8,128)(2,1)S(1)}, bf16[16,192,128]{2,1,0:T(8,128)(2,1)S(1)}, bf16[18,576,128]{2,1,0:T(8,128)(2,1)S(1)}) custom-call(bf16[1,8,192,128]{3,2,1,0:T(8,128)(2,1)} %bitcast.6, f32[1,192]{1,0:T(1,128)} %bitcast.7, f32[1,192]{1,0:T(1,128)} %bitcast.8, ...), custom_call_target="tpu_custom_call" | custom-call | tf_op jit(solution)/shard_map/pallas_call | solution.py:434
  14.1 1.4 %shard_map.65 = bf16[1,16,192,128]{3,2,1,0:T(8,128)(2,1)} custom-call(bf16[1,16,192,128]{3,2,1,0:T(8,128)(2,1)S(1)} %get-tuple-element.9.ready, bf16[192,1728]{1,0:T(8,128)(2,1)S(1)} %get-tuple-element.10.weight, bf16[16,192,128]{2,1,0:T(8,128)(2,1)S(1)} %get-tuple-element.11.skip, bf16[18,576,128]{2,1,0:T(8,128)(2,1)S(1)} %get-tuple-element.12.field3), custom_call_target="tpu_custom_call" | custom-call | tf_op jit(solution)/shard_map/pallas_call | solution.py:463
where the time goes:
time: 15.7 us; the launch traced here: 15.5 us
  Pallas kernels  15.5 us (99%)
    pallas_call x1, Pallas kernels, local(): pl.pallas_call(functools.partial(block_kernel, ha_count), out_shape=[pltp...  14.1 us
    pallas_call x1, Pallas kernels, local(): pl.pallas_call(finish_kernel, out_shape=jax.ShapeDtypeStruct(result[0].sh...  1.42 us

commit v1 on v0

--- a/solution.py
+++ b/solution.py
@@ -181,7 +181,7 @@
             return jnp.where(has_below, value, jnp.zeros_like(value))
         return value
 
-    def upsample(plane, count, plan, apart):
+    def upsample(plane, count, plan):
         extras = []
         parts = {}
 
@@ -194,14 +194,10 @@
                 up_w[rp, cp], jnp.concatenate(pieces, axis=0), preferred_element_type=f32
             ).astype(bf16)
 
-        if apart:
-            for cp in range(2):
-                for rp in range(2):
-                    phase(rp, cp)
+        for cp in range(2):
+            for rp in range(2):
+                phase(rp, cp)
         for rp in range(2):
-            if not apart:
-                phase(rp, 0)
-                phase(rp, 1)
             extra = None
             for k in (count - 1, *range(count - 1)):
                 cut = slice(k * width, (k + 1) * width)
@@ -353,15 +349,14 @@
 
     own.wait()
     inner_pairs(mine)
-    raw_copies[0].wait()
+    for item in raw_copies:
+        item.wait()
     turn(0, one_w)
-    raw_copies[1].wait()
+    for item in up_copies:
+        item.wait()
     side.wait()
     inner_pairs(theirs)
-    for item in up_copies:
-        item.wait()
-
-    extras = upsample(inner_plane, h, inner_plan, False)
+    extras = upsample(inner_plane, h, inner_plan)
     slims = slim_near_far(extras[1], extras[0], SLOT)
     slims.append(slim_edges([(r, r - 3) for r in range(3, 2 * rows + 1)]))
     for n in range(3):
@@ -375,11 +370,11 @@
     outer_pairs(mine)
     conv_two(range(3, 7))
     conv_two(range(7, 11))
-    conv_two(range(11, 2 * rows - 3))
     arrived(0)
     arrived(1)
+    conv_two(range(11, 2 * rows - 3))
     outer_pairs(theirs)
-    extras = upsample(outer_plane, 2, outer_plan, True)
+    extras = upsample(outer_plane, 2, outer_plan)
     slims = slim_near_far(extras[0], extras[1], width - SLOT)
     slims.append(slim_edges([
         *((r, r) for r in range(5)), *((2 * rows - 1 + r, 5 + r) for r in range(5))

time: 15.7 us -> 15.3 us (0.975)
  Pallas kernels: 15.5 us -> 15.2 us
    pallas_call x1, Pallas kernels: 14.1 us -> 13.7 us  [local(): pl.pallas_call(functools.partial(block_kernel, ha_count), out_shape=[pltp...]
where the time goes in v1:
time: 15.3 us; the launch traced here: 15.2 us
  Pallas kernels  15.2 us (99%)
    pallas_call x1, Pallas kernels, local(): pl.pallas_call(functools.partial(block_kernel, ha_count), out_shape=[pltp...  13.7 us
    pallas_call x1, Pallas kernels, local(): pl.pallas_call(finish_kernel, out_shape=jax.ShapeDtypeStruct(result[0].sh...  1.42 us

profile of v1, /device:TPU:0, one launch (start us, length us, event | category | flops | bytes accessed | tf_op | source)
XLA Modules:
  0.0 15.2 jit_solution(10123318284461281390)
XLA Ops:
  0.0 13.7 %shard_map.64 = (bf16[1,16,192,128]{3,2,1,0:T(8,128)(2,1)S(1)}, bf16[192,1728]{1,0:T(8,128)(2,1)S(1)}, bf16[16,192,128]{2,1,0:T(8,128)(2,1)S(1)}, bf16[18,576,128]{2,1,0:T(8,128)(2,1)S(1)}) custom-call(bf16[1,8,192,128]{3,2,1,0:T(8,128)(2,1)} %bitcast.6, f32[1,192]{1,0:T(1,128)} %bitcast.7, f32[1,192]{1,0:T(1,128)} %bitcast.8, ...), custom_call_target="tpu_custom_call" | custom-call | tf_op jit(solution)/shard_map/pallas_call | solution.py:429
  13.7 1.4 %shard_map.65 = bf16[1,16,192,128]{3,2,1,0:T(8,128)(2,1)} custom-call(bf16[1,16,192,128]{3,2,1,0:T(8,128)(2,1)S(1)} %get-tuple-element.9.ready, bf16[192,1728]{1,0:T(8,128)(2,1)S(1)} %get-tuple-element.10.weight, bf16[16,192,128]{2,1,0:T(8,128)(2,1)S(1)} %get-tuple-element.11.skip, bf16[18,576,128]{2,1,0:T(8,128)(2,1)S(1)} %get-tuple-element.12.field3), custom_call_target="tpu_custom_call" | custom-call | tf_op jit(solution)/shard_map/pallas_call | solution.py:458

commit v2 on v1

--- a/solution.py
+++ b/solution.py
@@ -369,9 +369,9 @@
     forward(1)
     outer_pairs(mine)
     conv_two(range(3, 7))
-    conv_two(range(7, 11))
     arrived(0)
     arrived(1)
+    conv_two(range(7, 11))
     conv_two(range(11, 2 * rows - 3))
     outer_pairs(theirs)
     extras = upsample(outer_plane, 2, outer_plan)
@@ -388,7 +388,7 @@
         old = pltpu.roll(slim[n], width - (2 * rows - 9) * SLOT, 1)
         slims[n] = jnp.where((spot == 5) | (spot == 6), old, value)
     conv_one(
-        ((0, 1, 2, 2 * rows - 1), (None, 2 * rows, 2 * rows + 1)), slims,
+        ((0, 1, 2, 2 * rows - 1, 2 * rows, 2 * rows + 1, None),), slims,
         lambda r: r + 1 if r < 3 else r - (2 * rows - 7)
     )
 

time: 15.3 us -> 15.3 us (level)
  no operation moved by 1% of the time
where the time goes in v2:
time: 15.3 us; the launch traced here: 15.1 us
  Pallas kernels  15.1 us (99%)
    pallas_call x1, Pallas kernels, local(): pl.pallas_call(functools.partial(block_kernel, ha_count), out_shape=[pltp...  13.7 us
    pallas_call x1, Pallas kernels, local(): pl.pallas_call(finish_kernel, out_shape=jax.ShapeDtypeStruct(result[0].sh...  1.42 us

profile of v2, /device:TPU:0, one launch (start us, length us, event | category | flops | bytes accessed | tf_op | source)
XLA Modules:
  0.0 15.1 jit_solution(17444435431573657221)
XLA Ops:
  0.0 13.7 %shard_map.64 = (bf16[1,16,192,128]{3,2,1,0:T(8,128)(2,1)S(1)}, bf16[192,1728]{1,0:T(8,128)(2,1)S(1)}, bf16[16,192,128]{2,1,0:T(8,128)(2,1)S(1)}, bf16[18,576,128]{2,1,0:T(8,128)(2,1)S(1)}) custom-call(bf16[1,8,192,128]{3,2,1,0:T(8,128)(2,1)} %bitcast.6, f32[1,192]{1,0:T(1,128)} %bitcast.7, f32[1,192]{1,0:T(1,128)} %bitcast.8, ...), custom_call_target="tpu_custom_call" | custom-call | tf_op jit(solution)/shard_map/pallas_call | solution.py:429
  13.7 1.4 %shard_map.65 = bf16[1,16,192,128]{3,2,1,0:T(8,128)(2,1)} custom-call(bf16[1,16,192,128]{3,2,1,0:T(8,128)(2,1)S(1)} %get-tuple-element.9.ready, bf16[192,1728]{1,0:T(8,128)(2,1)S(1)} %get-tuple-element.10.weight, bf16[16,192,128]{2,1,0:T(8,128)(2,1)S(1)} %get-tuple-element.11.skip, bf16[18,576,128]{2,1,0:T(8,128)(2,1)S(1)} %get-tuple-element.12.field3), custom_call_target="tpu_custom_call" | custom-call | tf_op jit(solution)/shard_map/pallas_call | solution.py:458
